TPU v7x, 32 devices: a whole 2x2x4 slice. The times are simulated.
32 devices in a mesh: ctx: 16 (over z, y, core), ch: 2 (over x).
Axes of the slice: x: 2, y: 2, z: 4, core: 2. Of those that a mesh axis runs over, the one named last changes fastest.
Arguments:
- projections: bfloat16 [3, 2048, 8192], P(None, 'ctx', 'ch'), may hold values from -150 to 150
- grouped_short_filters: float32 [3, 7, 512], P(None, None, 'ch'), may hold values from -2 to 2
- long_filter: float32 [2048, 8192], P('ctx', 'ch'), may hold values from 0 to 0.5
- norm_gain: float32 [8192], P('ch'), may hold values from 0.1 to 1.9
- out_grad: bfloat16 [2048, 8192], P('ctx', 'ch'), may hold values from -6 to 6
Outputs:
- output: bfloat16 [2048, 8192], P('ctx', 'ch')
- proj_grads: bfloat16 [3, 2048, 8192], P(None, 'ctx', 'ch')
- short_grads: float32 [3, 7, 512], P(None, None, 'ch')
- long_grad: float32 [2048, 8192], P('ctx', 'ch')
- gain_grad: float32 [8192], P('ch')
All inputs are finite; a program needn't handle non-finite values.
Results may differ from a plain program's by a relative error of at most 0.0064.
Values may be sent and summed in bfloat16 or wider, within the bound.
No kernel may reach another device: no remote copies, remote signals or barrier semaphores. Data moves between devices by JAX's collectives and lax.ppermute only.
A program may use at most 128 MiB of HBM per device.

v0:
```python
import math
import jax
import jax.numpy as jnp
from jax import lax
from jax.sharding import PartitionSpec as P

D = 8192
GROUP = 16
KS = 7
epsilon = 1e-05


def passed_along(block, axis, distance):
    devices = range(lax.axis_size(axis))
    route = [(i - distance, i) for i in devices if i - distance in devices]
    return lax.ppermute(block, axis, route)


def contract(form, left, right):
    return jnp.einsum(form, left, right, precision=lax.Precision.HIGHEST)


def factor_sizes(period):
    inner_len = 1
    while 2 * inner_len * (2 * inner_len) <= period and period % (4 * inner_len) == 0:
        inner_len = inner_len * 2
    return (period // inner_len, inner_len)


def dft_tables(order):
    ordinal_list = jnp.arange(order, dtype=jnp.int32)
    phases = (ordinal_list[:, None] * ordinal_list[None, :] % order).astype(jnp.float32) * (
        2.0 * math.pi / order
    )
    return (jnp.cos(phases), jnp.sin(phases))


def make_tables(outer_len, inner_len):
    period = outer_len * inner_len
    cos_a, sin_a = dft_tables(outer_len)
    cos_b, sin_b = dft_tables(inner_len)
    row_ids = jnp.arange(outer_len, dtype=jnp.int32)[:, None]
    col_ids = jnp.arange(inner_len, dtype=jnp.int32)[None, :]
    phases = (row_ids * col_ids % period).astype(jnp.float32) * (2.0 * math.pi / period)
    return (cos_a, sin_a, cos_b, sin_b, jnp.cos(phases), jnp.sin(phases))


def forward_spectrum(signal, tables):
    cos_a, sin_a, cos_b, sin_b, tw_cos, tw_sin = tables
    outer_len = cos_a.shape[0]
    inner_len = cos_b.shape[0]
    half_len = outer_len // 2
    channels = signal.shape[0]
    grid_rows = signal.reshape(channels, half_len, inner_len)
    real_a = contract("cnb,kn->ckb", grid_rows, cos_a[:, :half_len])
    imag_a = -contract("cnb,kn->ckb", grid_rows, sin_a[:, :half_len])
    real_t = real_a * tw_cos + imag_a * tw_sin
    imag_t = imag_a * tw_cos - real_a * tw_sin
    real_s = contract("ckb,bm->ckm", real_t, cos_b) + contract("ckb,bm->ckm", imag_t, sin_b)
    imag_s = contract("ckb,bm->ckm", imag_t, cos_b) - contract("ckb,bm->ckm", real_t, sin_b)
    return (real_s, imag_s)


def inverse_signal(real_s, imag_s, tables):
    cos_a, sin_a, cos_b, sin_b, tw_cos, tw_sin = tables
    outer_len = cos_a.shape[0]
    inner_len = cos_b.shape[0]
    half_len = outer_len // 2
    channels = real_s.shape[0]
    real_z = contract("ckb,bm->ckm", real_s, cos_b) - contract("ckb,bm->ckm", imag_s, sin_b)
    imag_z = contract("ckb,bm->ckm", imag_s, cos_b) + contract("ckb,bm->ckm", real_s, sin_b)
    real_t = real_z * tw_cos - imag_z * tw_sin
    imag_t = imag_z * tw_cos + real_z * tw_sin
    signal = contract("ckb,kn->cnb", real_t, cos_a[:, :half_len]) - contract(
        "ckb,kn->cnb", imag_t, sin_a[:, :half_len]
    )
    scale_back = 1.0 / (outer_len * inner_len)
    return (signal * scale_back).reshape(channels, half_len * inner_len)


def channel_sum(values):
    return lax.psum(values, "ch")


def on_device(projections, grouped_short_filters, long_filter, norm_gain, out_grad):
    tokens = projections.shape[1]
    spread = lax.axis_size("ctx")
    length = tokens * spread
    outer_len, inner_len = factor_sizes(2 * length)
    tables = make_tables(outer_len, inner_len)
    per_chan = jnp.repeat(grouped_short_filters, GROUP, axis=2)
    edge_rows = passed_along(projections[:, tokens - (KS - 1) :, :], "ctx", 1)
    extended = jnp.concatenate([edge_rows, projections], axis=1)
    conv_sum = jnp.zeros(projections.shape, jnp.float32)
    for tap_idx in range(KS):
        window = extended[:, KS - 1 - tap_idx : KS - 1 - tap_idx + tokens, :].astype(jnp.float32)
        conv_sum = conv_sum + per_chan[:, tap_idx, None, :] * window
    features = lax.optimization_barrier(conv_sum.astype(jnp.bfloat16))
    gate_feat = features[0].astype(jnp.float32)
    key_feat = features[1].astype(jnp.float32)
    value_feat = features[2].astype(jnp.float32)
    mixed_in = key_feat * value_feat
    chan_h = lax.all_to_all(long_filter.T, "ctx", split_axis=0, concat_axis=1, tiled=True)
    chan_u = lax.all_to_all(mixed_in.T, "ctx", split_axis=0, concat_axis=1, tiled=True)
    real_u, imag_u = forward_spectrum(chan_u, tables)
    real_h, imaginary_filter = forward_spectrum(chan_h, tables)
    prod_r = real_u * real_h - imag_u * imaginary_filter
    prod_i = real_u * imaginary_filter + imag_u * real_h
    chan_z = inverse_signal(prod_r, prod_i, tables)
    conv_out = lax.all_to_all(chan_z, "ctx", split_axis=1, concat_axis=0, tiled=True).T
    gated_out = gate_feat * conv_out
    sq_total = channel_sum(jnp.sum(gated_out * gated_out, axis=1))
    rscale = lax.rsqrt(sq_total / D + epsilon)
    normed = gated_out * rscale[:, None]
    output = (normed * norm_gain).astype(jnp.bfloat16)
    gradient_float = out_grad.astype(jnp.float32)
    scaled = gradient_float * norm_gain
    inner_total = channel_sum(jnp.sum(scaled * normed, axis=1))
    grad_gated = rscale[:, None] * (scaled - normed * (inner_total / D)[:, None])
    gain_part = jnp.sum(gradient_float * normed, axis=0)
    grad_conv = grad_gated * gate_feat
    grad_gate = grad_gated * conv_out
    cotangent_gate_input = lax.all_to_all(
        grad_conv.T, "ctx", split_axis=0, concat_axis=1, tiled=True
    )
    real_d, imag_d = forward_spectrum(cotangent_gate_input, tables)
    back_r = real_h * real_d + imaginary_filter * imag_d
    back_i = real_h * imag_d - imaginary_filter * real_d
    filt_r = real_u * real_d + imag_u * imag_d
    filt_i = real_u * imag_d - imag_u * real_d
    chan_du = inverse_signal(back_r, back_i, tables)
    chan_dh = inverse_signal(filt_r, filt_i, tables)
    mix_back = lax.all_to_all(chan_du, "ctx", split_axis=1, concat_axis=0, tiled=True)
    filt_back = lax.all_to_all(chan_dh, "ctx", split_axis=1, concat_axis=0, tiled=True)
    grad_mix = mix_back.T
    long_grad = filt_back.T
    grad_feats = jnp.stack([grad_gate, grad_mix * value_feat, grad_mix * key_feat])
    next_rows = passed_along(grad_feats[:, : KS - 1, :], "ctx", -1)
    cotangent_widened = jnp.concatenate([grad_feats, next_rows], axis=1)
    grad_in = jnp.zeros(grad_feats.shape, jnp.float32)
    tap_terms = []
    local_width = projections.shape[2]
    for tap_idx in range(KS):
        grad_in = (
            grad_in
            + per_chan[:, tap_idx, None, :] * cotangent_widened[:, tap_idx : tap_idx + tokens, :]
        )
        window = extended[:, KS - 1 - tap_idx : KS - 1 - tap_idx + tokens, :].astype(jnp.float32)
        tap_prod = jnp.sum(grad_feats * window, axis=1)
        tap_terms.append(jnp.sum(tap_prod.reshape(3, local_width // GROUP, GROUP), axis=2))
    filt_part = jnp.stack(tap_terms, axis=1)
    gain_grad, short_grads = lax.psum((gain_part, filt_part), "ctx")
    return (output, grad_in.astype(jnp.bfloat16), short_grads, long_grad, gain_grad)


def solution(mesh):
    in_specs = (P(None, "ctx", "ch"), P(None, None, "ch"), P("ctx", "ch"), P("ch"), P("ctx", "ch"))
    out_specs = (P("ctx", "ch"), P(None, "ctx", "ch"), P(None, None, "ch"), P("ctx", "ch"), P("ch"))
    return jax.shard_map(
        on_device, mesh=mesh, in_specs=in_specs, out_specs=out_specs, check_vma=False
    )
```

profile of v0, /device:TPU:0, one launch (start us, length us, event | category | flops | bytes accessed | tf_op | source)
XLA Modules:
  0.0 693.5 jit_solution(7625350813707377017)
XLA Ops:
  8.4 6.6 all-to-all-start.1
  27.5 26.1 %fusion.6 = bf16[3,128,4096]{1,2,0:T(8,128)(2,1)S(1)} fusion(bf16[3,128,4096]{1,2,0:T(8,128)(2,1)S(1)} %copy.105, f32[3,4096]{1,0:T(4,128)S(1)} %get-tuple-element.72, f32[3,4096]{1,0:T(4,128)S(1)} %get-tuple-element.73, f32[3,4096]{1,0:T(4,128)S(1)} %get-tuple-element.74, f32[3,4096]{1,0:T(4,128)S(1)} %get-tuple-element.75, ...), kind=kLoop, calls=%fused_computation.31 | loop fusion | flops 61341696 | bytes 6782976 | tf_op jit(solution)/shard_map/convert_element_type | solution.py:98
  56.8 11.0 %all-to-all-start = ((f32[16,256,128]{2,1,0:T(8,128)}), f32[16,256,128]{2,1,0:T(8,128)}, u32[]{:S(2)}, u32[]{:S(2)}) async-start(f32[16,256,128]{2,1,0:T(8,128)} %bitcast.237), calls=%async_computation | async-start | bytes 4194304 | tf_op jit(solution)/shard_map/all_to_all | solution.py:104
  70.3 5.8 fusion.91
  76.2 5.8 fusion.93
  82.0 26.8 %all-to-all-done = f32[16,256,128]{2,1,0:T(8,128)} async-done(((f32[16,256,128]{2,1,0:T(8,128)}), f32[16,256,128]{2,1,0:T(8,128)}, u32[]{:S(2)}, u32[]{:S(2)}) %all-to-all-start) | async-done | bytes 2097184 | tf_op jit(solution)/shard_map/all_to_all | solution.py:104
  110.7 5.8 fusion.95
  116.5 9.0 %add_bitcast_fusion.1 = (f32[256,64,64]{0,1,2:T(8,128)S(1)}, f32[256,64,64]{0,1,2:T(8,128)S(1)}, f32[256,64,64]{0,1,2:T(8,128)S(1)}, f32[256,64,64]{0,1,2:T(8,128)S(1)}) fusion(f32[64,256,64]{1,0,2:T(8,128)} %fusion.93, f32[64,256,64]{1,0,2:T(8,128)} %fusion.91, f32[64,64]{0,1:T(8,128)S(1)} %get-tuple-element.78, f32[64,64]{0,1:T(8,128)S(1)} %get-tuple-element.79, ...), kind=kOutput, calls=%fused_computation.80 | convolution fusion | flops 417333248 | bytes 31539200 | tf_op jit(solution)/shard_map/cnb,kn->ckb/dot_general | solution.py:20
  125.5 6.4 fusion.41
  132.0 6.9 fusion.43
  138.9 7.2 %fusion.49 = f32[256,64,64]{0,2,1:T(8,128)} fusion(f32[256,64,64]{0,1,2:T(8,128)S(1)} %get-tuple-element.69), kind=kOutput, calls=%fused_computation.99 | convolution fusion | flops 805363712 | bytes 8388608 | tf_op jit(solution)/shard_map/ckb,bm->ckm/dot_general | solution.py:20
  146.1 6.5 fusion.51
  152.6 7.3 %fusion.73 = f32[256,64,64]{0,2,1:T(8,128)S(1)} fusion(f32[256,64,64]{0,2,1:T(8,128)S(1)} %fusion.41, f32[256,64,64]{0,1,2:T(8,128)S(1)} %get-tuple-element.49), kind=kOutput, calls=%fused_computation.125 | convolution fusion | flops 806412288 | bytes 12582912 | tf_op jit(solution)/shard_map/ckb,bm->ckm/dot_general | solution.py:20
  159.8 7.3 %fusion.70 = f32[256,64,64]{0,2,1:T(8,128)} fusion(f32[256,64,64]{0,2,1:T(8,128)S(1)} %fusion.43, f32[256,64,64]{0,1,2:T(8,128)S(1)} %get-tuple-element.49), kind=kOutput, calls=%fused_computation.124 | convolution fusion | flops 806412288 | bytes 12582912 | tf_op jit(solution)/shard_map/ckb,bm->ckm/dot_general | solution.py:20
  167.1 7.2 %fusion.64 = f32[256,64,64]{0,2,1:T(8,128)} fusion(f32[256,64,64]{0,2,1:T(8,128)S(1)} %fusion.51, f32[256,64,64]{0,1,2:T(8,128)S(1)} %get-tuple-element.70), kind=kOutput, calls=%fused_computation.122 | convolution fusion | flops 806412288 | bytes 12582912 | tf_op jit(solution)/shard_map/ckb,bm->ckm/dot_general | solution.py:20
  174.3 11.9 %multiply_add_fusion.5 = (f32[256,64,64]{0,2,1:T(8,128)S(1)}, f32[256,64,64]{0,2,1:T(8,128)S(1)}, f32[256,64,64]{0,2,1:T(8,128)}) fusion(f32[256,64,64]{0,2,1:T(8,128)} %fusion.70, f32[256,64,64]{0,2,1:T(8,128)} %fusion.64, f32[256,64,64]{0,2,1:T(8,128)S(1)} %fusion.73, f32[256,64,64]{0,2,1:T(8,128)} %fusion.49, f32[256,64,64]{0,1,2:T(8,128)S(1)} %get-tuple-element.70), kind=kOutput, calls=%fused_computation.77 | convolution fusion | flops 812703744 | bytes 33554432 | tf_op jit(solution)/shard_map/ckb,bm->ckm/dot_general | solution.py:20
  195.0 4.8 convolution_subtract_fusion.2
  199.8 6.6 multiply_subtract_fusion.4
  210.9 4.9 multiply_bitcast_fusion.2
  218.3 11.3 %all-to-all-start.2 = ((f32[256,16,128]{0,2,1:T(8,128)}), f32[256,16,128]{0,2,1:T(8,128)}, u32[]{:S(2)}, u32[]{:S(2)}) async-start(f32[256,16,128]{0,2,1:T(8,128)} %bitcast.20), calls=%async_computation.2 | async-start | bytes 4194304 | tf_op jit(solution)/shard_map/all_to_all | solution.py:110
  232.0 38.6 %all-to-all-done.2 = f32[256,16,128]{0,2,1:T(8,128)} async-done(((f32[256,16,128]{0,2,1:T(8,128)}), f32[256,16,128]{0,2,1:T(8,128)}, u32[]{:S(2)}, u32[]{:S(2)}) %all-to-all-start.2) | async-done | bytes 2097184 | tf_op jit(solution)/shard_map/all_to_all | solution.py:110
  275.6 5.0 psum.28
  283.4 4.9 psum.29
  291.0 58.2 %all_to_all.105 = f32[16,256,128]{2,1,0:T(8,128)} all-to-all(f32[16,256,128]{2,1,0:T(8,128)S(1)} %bitcast.235), channel_id=1, replica_groups=mesh['ctx'=16,'ch'=2] {'ctx'}, dimensions={0} | all-to-all | bytes 4194304 | tf_op jit(solution)/shard_map/all_to_all | solution.py:123
  352.3 6.3 fusion.87
  358.6 6.0 add_bitcast_fusion
  364.6 6.9 fusion.33
  371.5 7.2 %fusion.35 = f32[256,64,64]{0,2,1:T(8,128)} fusion(f32[256,64,64]{0,1,2:T(8,128)S(1)} %get-tuple-element.46), kind=kOutput, calls=%fused_computation.85 | convolution fusion | flops 805363712 | bytes 8388608 | tf_op jit(solution)/shard_map/ckb,bm->ckm/dot_general | solution.py:20
  378.7 7.3 %fusion.79 = f32[256,64,64]{0,2,1:T(8,128)} fusion(f32[256,64,64]{0,2,1:T(8,128)S(1)} %fusion.33, f32[256,64,64]{0,1,2:T(8,128)S(1)} %get-tuple-element.45), kind=kOutput, calls=%fused_computation.127 | convolution fusion | flops 806412288 | bytes 12582912 | tf_op jit(solution)/shard_map/ckb,bm->ckm/dot_general | solution.py:20
  386.0 21.5 %multiply_subtract_fusion.1 = (f32[256,64,64]{0,2,1:T(8,128)}, f32[256,64,64]{0,2,1:T(8,128)}, f32[256,64,64]{0,2,1:T(8,128)}, f32[256,64,64]{0,2,1:T(8,128)}) fusion(f32[256,64,64]{0,2,1:T(8,128)} %get-tuple-element.71, f32[256,64,64]{0,2,1:T(8,128)} %fusion.64, f32[256,64,64]{0,2,1:T(8,128)} %fusion.79, f32[256,64,64]{0,2,1:T(8,128)} %copy-done.9, ...), kind=kOutput, calls=%fused_computation.67 | convolution fusion | flops 818995200 | bytes 46137344 | tf_op jit(solution)/shard_map/ckb,bm->ckm/dot_general | solution.py:20
  407.5 8.4 %fusion.121 = f32[256,64,64]{0,2,1:T(8,128)} fusion(f32[256,64,64]{0,2,1:T(8,128)} %get-tuple-element.31), kind=kOutput, calls=%fused_computation.188 | convolution fusion | flops 805363712 | bytes 8388608 | tf_op jit(solution)/shard_map/ckb,bm->ckm/dot_general | solution.py:20
  420.1 5.7 convolution_subtract_fusion
  434.3 5.6 convolution_subtract_fusion.1
  439.8 5.8 convolution_add_fusion.1
  445.6 11.7 %multiply_subtract_fusion = (f32[256,64,64]{0,2,1:T(8,128)}, f32[256,64,64]{0,2,1:T(8,128)}, f32[256,64,64]{0,2,1:T(8,128)}, f32[256,64,64]{0,2,1:T(8,128)S(1)}) fusion(f32[256,64,64]{0,2,1:T(8,128)} %convolution_subtract_fusion, f32[64,64]{1,0:T(8,128)S(1)} %copy.124, f32[64,64]{1,0:T(8,128)S(1)} %copy.123, f32[256,64,64]{0,2,1:T(8,128)} %convolution_subtract_fusion.1, ...), kind=kOutput, calls=%fused_computation.66 | convolution fusion | flops 818995200 | bytes 37781504 | tf_op jit(solution)/shard_map/ckb,bm->ckm/dot_general | solution.py:20
  457.3 7.4 %fusion.25 = f32[32,256,64]{1,0,2:T(8,128)S(1)} fusion(f32[256,64,64]{0,2,1:T(8,128)} %get-tuple-element.67, f32[64,64]{0,1:T(8,128)S(1)} %fusion.148), kind=kOutput, calls=%fused_computation.57 | convolution fusion | flops 402653184 | bytes 6307840 | tf_op jit(solution)/shard_map/ckb,kn->cnb/dot_general | solution.py:20
  464.7 4.7 multiply_bitcast_fusion.1
  471.9 5.4 all-to-all-start.4
  478.6 7.1 %fusion.21 = f32[32,256,64]{1,0,2:T(8,128)S(1)} fusion(f32[256,64,64]{0,2,1:T(8,128)} %get-tuple-element.42, f32[64,64]{0,1:T(8,128)S(1)} %fusion.148), kind=kOutput, calls=%fused_computation.53 | convolution fusion | flops 402653184 | bytes 6307840 | tf_op jit(solution)/shard_map/ckb,kn->cnb/dot_general | solution.py:20
  485.7 4.7 multiply_bitcast_fusion
  493.0 25.3 %all-to-all-done.4 = f32[256,16,128]{0,2,1:T(8,128)} async-done(((f32[256,16,128]{0,2,1:T(8,128)}), f32[256,16,128]{0,2,1:T(8,128)}, u32[]{:S(2)}, u32[]{:S(2)}) %all-to-all-start.4) | async-done | bytes 2097184 | tf_op jit(solution)/shard_map/all_to_all | solution.py:133
  518.3 11.5 %all-to-all-start.5 = ((f32[256,16,128]{0,2,1:T(8,128)}), f32[256,16,128]{0,2,1:T(8,128)}, u32[]{:S(2)}, u32[]{:S(2)}) async-start(f32[256,16,128]{0,2,1:T(8,128)} %bitcast.236), calls=%async_computation.5 | async-start | bytes 4194304 | tf_op jit(solution)/shard_map/all_to_all | solution.py:134
  538.0 21.9 %fusion.12 = (f32[3,4096]{1,0:T(4,128)S(1)}, f32[3,4096]{1,0:T(4,128)S(1)}, f32[3,4096]{1,0:T(4,128)S(1)}, f32[3,4096]{1,0:T(4,128)S(1)}, f32[3,4096]{1,0:T(4,12...) fusion(bf16[3,128,4096]{1,2,0:T(8,128)(2,1)S(1)} %copy-done.13, bf16[3,6,4096]{1,2,0:T(8,128)(2,1)S(1)} %copy-done.14, ...), kind=kLoop, calls=%fused_computation.37 | loop fusion | flops 64401408 | bytes 9928704 | tf_op jit(solution)/shard_map/reduce_sum | solution.py:149
  562.1 5.3 pad_maximum_fusion.1
  579.4 65.7 %all-reduce = (f32[3,7,256]{2,0,1:T(4,128)S(1)}, f32[4096]{0:T(1024)}) all-reduce(f32[3,7,256]{2,0,1:T(4,128)S(1)} %constant_dynamic-update-slice_fusion, f32[4096]{0:T(1024)S(1)} %get-tuple-element.27), channel_id=1, replica_groups=mesh['ctx'=16,'ch'=2] {'ctx'}, use_global_device_ids=true, to_apply=%region_18.19 | all-reduce | flops 9472 | bytes 75776 | tf_op jit(solution)/shard_map/psum | solution.py:152
  649.7 10.6 %pad_maximum_fusion = f32[3,134,4096]{1,2,0:T(8,128)} fusion(f32[3,6,4096]{1,2,0:T(8,128)} %copy.142, f32[1,128,4096]{1,2,0:T(8,128)} %copy-done.2, f32[1,128,4096]{1,2,0:T(8,128)} %copy-done, f32[1,128,4096]{1,2,0:T(8,128)S(1)} %bitcast.226), kind=kLoop, calls=%fused_computation | loop fusion | flops 4939776 | bytes 13172736 | tf_op jit(solution)/shard_map/concatenate | solution.py:139
  660.4 28.2 %fusion.15 = bf16[3,128,4096]{1,2,0:T(8,128)(2,1)} fusion(f32[3,134,4096]{1,2,0:T(8,128)} %pad_maximum_fusion, f32[3,4096]{1,0:T(4,128)S(1)} %copy-done.18, f32[3,4096]{1,0:T(4,128)S(1)} %copy-done.20, f32[3,4096]{1,0:T(4,128)S(1)} %copy-done.22, f32[3,4096]{1,0:T(4,128)S(1)} %copy-done.24, f32[3,4096]{1,0:T(4,128)S(1)} %copy-done.26, ...), kind=kLoop, calls=%fused_computation.41 | loop fusion | flops 25165824 | bytes 47529984 | tf_op jit(solution)/shard_map/convert_element_type | solution.py:153
  688.6 4.6 copy.148
  (135 shorter events, 105.5 us)
Async XLA Ops:
  2.3 12.7 %copy-start.31 = (f32[3,7,256]{2,1,0:T(8,128)S(1)}, f32[3,7,256]{2,1,0:T(8,128)}, u32[]{:S(2)}) copy-start(f32[3,7,256]{2,1,0:T(8,128)} %param.6) | copy-start | bytes 64516
  2.3 21.6 %collective-permute-start = (bf16[3,6,4096]{2,1,0:T(8,128)(2,1)}, bf16[3,6,4096]{2,1,0:T(8,128)(2,1)}, u32[]{:S(2)}, u32[]{:S(2)}) collective-permute-start(bf16[3,6,4096]{2,1,0:T(8,128)(2,1)} %slice.123), channel_id=1, source_target_pairs={{0,2},{2,4},{4,6},{6,8},{8,10},{10,12},{12,14},{14,16},{16,18},{18... | collective-permute-start | bytes 442376 | tf_op jit(solution)/shard_map/ppermute | solution.py:16
  8.4 48.4 %all-to-all-start.1 = ((f32[16,256,128]{2,1,0:T(8,128)}), f32[16,256,128]{2,1,0:T(8,128)}, u32[]{:S(2)}, u32[]{:S(2)}) async-start(f32[16,256,128]{2,1,0:T(8,128)} %bitcast.14), calls=%async_computation.1 | async-start | bytes 4194304 | tf_op jit(solution)/shard_map/all_to_all | solution.py:103
  18.4 9.1 %copy-start.17 = (f32[3,4096]{1,0:T(4,128)}, f32[3,4096]{1,0:T(4,128)S(1)}, u32[]{:S(2)}) copy-start(f32[3,4096]{1,0:T(4,128)S(1)} %get-tuple-element.72) | copy-start | bytes 147460
  18.4 9.1 %copy-start.19 = (f32[3,4096]{1,0:T(4,128)}, f32[3,4096]{1,0:T(4,128)S(1)}, u32[]{:S(2)}) copy-start(f32[3,4096]{1,0:T(4,128)S(1)} %get-tuple-element.73) | copy-start | bytes 147460
  18.5 9.0 %copy-start.21 = (f32[3,4096]{1,0:T(4,128)}, f32[3,4096]{1,0:T(4,128)S(1)}, u32[]{:S(2)}) copy-start(f32[3,4096]{1,0:T(4,128)S(1)} %get-tuple-element.74) | copy-start | bytes 147460
  18.5 9.0 %copy-start.23 = (f32[3,4096]{1,0:T(4,128)}, f32[3,4096]{1,0:T(4,128)S(1)}, u32[]{:S(2)}) copy-start(f32[3,4096]{1,0:T(4,128)S(1)} %get-tuple-element.75) | copy-start | bytes 147460
  18.6 8.9 %copy-start.25 = (f32[3,4096]{1,0:T(4,128)}, f32[3,4096]{1,0:T(4,128)S(1)}, u32[]{:S(2)}) copy-start(f32[3,4096]{1,0:T(4,128)S(1)} %get-tuple-element.76) | copy-start | bytes 147460
  18.6 8.9 %copy-start.27 = (f32[3,4096]{1,0:T(4,128)}, f32[3,4096]{1,0:T(4,128)S(1)}, u32[]{:S(2)}) copy-start(f32[3,4096]{1,0:T(4,128)S(1)} %get-tuple-element.77) | copy-start | bytes 147460
  22.1 31.4 %copy-start.12 = (bf16[3,128,4096]{1,2,0:T(8,128)(2,1)}, bf16[3,128,4096]{1,2,0:T(8,128)(2,1)S(1)}, u32[]{:S(2)}) copy-start(bf16[3,128,4096]{1,2,0:T(8,128)(2,1)S(1)} %copy.105) | copy-start | bytes 9437188
  53.6 1.7 copy-start.10
  56.8 52.0 %all-to-all-start = ((f32[16,256,128]{2,1,0:T(8,128)}), f32[16,256,128]{2,1,0:T(8,128)}, u32[]{:S(2)}, u32[]{:S(2)}) async-start(f32[16,256,128]{2,1,0:T(8,128)} %bitcast.237), calls=%async_computation | async-start | bytes 4194304 | tf_op jit(solution)/shard_map/all_to_all | solution.py:104
  159.8 14.5 %copy-start.9 = (f32[256,64,64]{0,2,1:T(8,128)}, f32[256,64,64]{0,2,1:T(8,128)S(1)}, u32[]{:S(2)}) copy-start(f32[256,64,64]{0,2,1:T(8,128)S(1)} %fusion.73) | copy-start | bytes 12582916
  218.3 52.3 %all-to-all-start.2 = ((f32[256,16,128]{0,2,1:T(8,128)}), f32[256,16,128]{0,2,1:T(8,128)}, u32[]{:S(2)}, u32[]{:S(2)}) async-start(f32[256,16,128]{0,2,1:T(8,128)} %bitcast.20), calls=%async_computation.2 | async-start | bytes 4194304 | tf_op jit(solution)/shard_map/all_to_all | solution.py:110
  229.6 43.9 %copy-start.11 = (bf16[3,128,4096]{1,2,0:T(8,128)(2,1)S(1)}, bf16[3,128,4096]{1,2,0:T(8,128)(2,1)}, u32[]{:S(2)}) copy-start(bf16[3,128,4096]{1,2,0:T(8,128)(2,1)} %copy-done.10) | copy-start | bytes 9437188
  232.0 48.6 %copy-start.30 = (f32[4096]{0:T(1024)S(1)}, f32[4096]{0:T(1024)}, u32[]{:S(2)}) copy-start(f32[4096]{0:T(1024)} %param.8) | copy-start | bytes 49156
  352.3 6.3 copy-start.15
  364.6 14.1 %copy-start.8 = (f32[256,64,64]{0,1,2:T(8,128)}, f32[256,64,64]{0,1,2:T(8,128)S(1)}, u32[]{:S(2)}) copy-start(f32[256,64,64]{0,1,2:T(8,128)S(1)} %get-tuple-element.45) | copy-start | bytes 12582916
  407.5 8.4 %copy-start.4 = (f32[256,64,64]{0,2,1:T(8,128)S(1)}, f32[256,64,64]{0,2,1:T(8,128)}, u32[]{:S(2)}) copy-start(f32[256,64,64]{0,2,1:T(8,128)} %get-tuple-element.32) | copy-start | bytes 12582916
  415.9 4.2 copy-start.7
  420.1 5.8 copy-start.5
  425.8 4.2 copy-start.6
  471.9 46.4 %all-to-all-start.4 = ((f32[256,16,128]{0,2,1:T(8,128)}), f32[256,16,128]{0,2,1:T(8,128)}, u32[]{:S(2)}, u32[]{:S(2)}) async-start(f32[256,16,128]{0,2,1:T(8,128)} %bitcast.238), calls=%async_computation.4 | async-start | bytes 4194304 | tf_op jit(solution)/shard_map/all_to_all | solution.py:133
  478.6 7.1 %copy-start.16 = (f32[256,64,64]{0,2,1:T(8,128)S(1)}, f32[256,64,64]{0,2,1:T(8,128)}, u32[]{:S(2)}) copy-start(f32[256,64,64]{0,2,1:T(8,128)} %get-tuple-element.41) | copy-start | bytes 12582916
  518.3 54.9 %all-to-all-start.5 = ((f32[256,16,128]{0,2,1:T(8,128)}), f32[256,16,128]{0,2,1:T(8,128)}, u32[]{:S(2)}, u32[]{:S(2)}) async-start(f32[256,16,128]{0,2,1:T(8,128)} %bitcast.236), calls=%async_computation.5 | async-start | bytes 4194304 | tf_op jit(solution)/shard_map/all_to_all | solution.py:134
  532.7 3.2 copy-start.13
  532.7 5.3 copy-start.14
  535.3 24.7 %copy-start = (f32[1,128,4096]{1,2,0:T(8,128)}, f32[1,128,4096]{1,2,0:T(8,128)S(1)}, u32[]{:S(2)}) copy-start(f32[1,128,4096]{1,2,0:T(8,128)S(1)} %get-tuple-element.58) | copy-start | bytes 6291460
  535.3 24.7 %copy-start.2 = (f32[1,128,4096]{1,2,0:T(8,128)}, f32[1,128,4096]{1,2,0:T(8,128)S(1)}, u32[]{:S(2)}) copy-start(f32[1,128,4096]{1,2,0:T(8,128)S(1)} %get-tuple-element.59) | copy-start | bytes 6291460
  571.9 73.8 %collective-permute-start.1 = (f32[3,6,4096]{2,1,0:T(8,128)S(1)}, f32[3,6,4096]{2,1,0:T(8,128)S(1)}, u32[]{:S(2)}, u32[]{:S(2)}) collective-permute-start(f32[3,6,4096]{2,1,0:T(8,128)S(1)} %copy.141), channel_id=1, source_target_pairs={{2,0},{4,2},{6,4},{8,6},{10,8},{12,10},{14,12},{16,14},{18,16},{20... | collective-permute-start | bytes 884744 | tf_op jit(solution)/shard_map/ppermute | solution.py:16
  649.6 10.7 %copy-start.1 = (f32[1,128,4096]{1,2,0:T(8,128)S(1)}, f32[1,128,4096]{1,2,0:T(8,128)}, u32[]{:S(2)}) copy-start(f32[1,128,4096]{1,2,0:T(8,128)} %copy-done) | copy-start | bytes 6291460
  649.6 10.7 %copy-start.3 = (f32[1,128,4096]{1,2,0:T(8,128)S(1)}, f32[1,128,4096]{1,2,0:T(8,128)}, u32[]{:S(2)}) copy-start(f32[1,128,4096]{1,2,0:T(8,128)} %copy-done.2) | copy-start | bytes 6291460
  649.6 10.7 %copy-start.18 = (f32[3,4096]{1,0:T(4,128)S(1)}, f32[3,4096]{1,0:T(4,128)}, u32[]{:S(2)}) copy-start(f32[3,4096]{1,0:T(4,128)} %copy-done.17) | copy-start | bytes 147460
  649.6 10.7 %copy-start.20 = (f32[3,4096]{1,0:T(4,128)S(1)}, f32[3,4096]{1,0:T(4,128)}, u32[]{:S(2)}) copy-start(f32[3,4096]{1,0:T(4,128)} %copy-done.19) | copy-start | bytes 147460
  649.7 10.7 %copy-start.22 = (f32[3,4096]{1,0:T(4,128)S(1)}, f32[3,4096]{1,0:T(4,128)}, u32[]{:S(2)}) copy-start(f32[3,4096]{1,0:T(4,128)} %copy-done.21) | copy-start | bytes 147460
  649.7 10.7 %copy-start.24 = (f32[3,4096]{1,0:T(4,128)S(1)}, f32[3,4096]{1,0:T(4,128)}, u32[]{:S(2)}) copy-start(f32[3,4096]{1,0:T(4,128)} %copy-done.23) | copy-start | bytes 147460
  649.7 10.7 %copy-start.26 = (f32[3,4096]{1,0:T(4,128)S(1)}, f32[3,4096]{1,0:T(4,128)}, u32[]{:S(2)}) copy-start(f32[3,4096]{1,0:T(4,128)} %copy-done.25) | copy-start | bytes 147460
  649.7 10.7 %copy-start.28 = (f32[3,4096]{1,0:T(4,128)S(1)}, f32[3,4096]{1,0:T(4,128)}, u32[]{:S(2)}) copy-start(f32[3,4096]{1,0:T(4,128)} %copy-done.27) | copy-start | bytes 147460
  649.7 10.7 %copy-start.29 = (f32[3,1,4096]{2,0,1:T(4,128)S(1)}, f32[3,1,4096]{2,0,1:T(4,128)}, u32[]{:S(2)}) copy-start(f32[3,1,4096]{2,0,1:T(4,128)} %copy.239) | copy-start | bytes 147460
where the time goes:
time: 699 us; the launch traced here: 693 us
  matrix products  245 us (35%)
  blocking collectives  134 us (19%)
  other arithmetic  105 us (15%)
  waiting for transfers between devices  90.7 us (13%)
  local copies, waits for them, and re-layouts  66.3 us (9%)
  starting transfers between devices  50.2 us (7%)
    dot_general x36, matrix products, contract(): return jnp.einsum(form, left, right, precision=lax.Precision.HIGHEST)  245 us
    psum x1, blocking collectives, on_device(): gain_grad, short_grads = lax.psum((gain_part, filt_part), 'ctx')  65.7 us
    all_to_all x1, blocking collectives, on_device(): lax.all_to_all(grad_conv.T, 'ctx', split_axis=0, concat_axis=1, tiled=True)  58.2 us
    all_to_all x1, waiting for transfers between devices, on_device(): lax.all_to_all(chan_z, 'ctx', split_axis=1, concat_axis=0, tiled=True)  38.6 us
    convert_element_type x1, other arithmetic, on_device(): grad_in.astype(jnp.bfloat16)  28.2 us
    all_to_all x1, waiting for transfers between devices, on_device(): lax.all_to_all(mixed_in.T, 'ctx', split_axis=0, concat_axis=1, tiled=True)  26.8 us
    convert_element_type x1, other arithmetic, on_device(): features = lax.optimization_barrier(conv_sum.astype(jnp.bfloat16))  26.1 us
    all_to_all x1, waiting for transfers between devices, on_device(): lax.all_to_all(chan_du, 'ctx', split_axis=1, concat_axis=0, tiled=True)  25.3 us
  transfers between devices with their start and end apart: 7, of which 3 were waited for; matrix products, arithmetic and copies ran while one was open for 17% of the time, Pallas kernels for 0%

commit v1 on v0

--- a/solution.py
+++ b/solution.py
@@ -101,7 +101,10 @@
     value_feat = features[2].astype(jnp.float32)
     mixed_in = key_feat * value_feat
     chan_h = lax.all_to_all(long_filter.T, "ctx", split_axis=0, concat_axis=1, tiled=True)
-    chan_u = lax.all_to_all(mixed_in.T, "ctx", split_axis=0, concat_axis=1, tiled=True)
+    chan_u = jnp.concatenate(
+        lax.all_to_all(jnp.stack(jnp.split(mixed_in.T, lax.axis_size("ctx"), axis=0)), "ctx", 0, 0),
+        axis=1,
+    )
     real_u, imag_u = forward_spectrum(chan_u, tables)
     real_h, imaginary_filter = forward_spectrum(chan_h, tables)
     prod_r = real_u * real_h - imag_u * imaginary_filter

time: 699 us -> 666 us (0.953)
  blocking collectives: 134 us -> 190 us
  other arithmetic: 105 us -> 51 us
  local copies, waits for them, and re-layouts: 66.3 us -> 37 us
  starting transfers between devices: 50.2 us -> 39.7 us
    all_to_all x0 -> x1, blocking collectives: none -> 58.4 us  [on_device(): lax.all_to_all(chan_z, 'ctx', split_axis=1, concat_axis=0, tiled=True)]
    all_to_all x2 -> x1, waiting for transfers between devices: 65.4 us -> 23.4 us  [on_device(): lax.all_to_all(jnp.stack(jnp.split(mixed_in.T, lax.axis_size('ctx'), axis...]
    all_to_all x1, waiting for transfers between devices: 0.01 us -> 24.5 us  [on_device(): lax.all_to_all(long_filter.T, 'ctx', split_axis=0, concat_axis=1, tiled=T...]
    all_to_all x1, waiting for transfers between devices: 0.01 us -> 20.9 us  [on_device(): lax.all_to_all(chan_dh, 'ctx', split_axis=1, concat_axis=0, tiled=True)]
    convert_element_type x1, other arithmetic: 26.1 us -> 7.1 us  [on_device(): features = lax.optimization_barrier(conv_sum.astype(jnp.bfloat16))]
    reduce_sum x1, other arithmetic: 21.9 us -> 8.49 us  [on_device(): tap_prod = jnp.sum(grad_feats * window, axis=1)]
    all_to_all x2 -> x1, starting transfers between devices: 22.3 us -> 11.7 us  [on_device(): lax.all_to_all(jnp.stack(jnp.split(mixed_in.T, lax.axis_size('ctx'), axis...]
    unnamed x81 -> x94, local copies, waits for them, and re-layouts: 24.7 us -> 14.2 us
  transfers between devices with their start and end apart: 7 -> 6, of which waited for: 3 -> 4; matrix products, arithmetic and copies ran while one was open for 17% -> 11% of each run, Pallas kernels for 0% -> 0%
where the time goes in v1:
time: 666 us; the launch traced here: 661 us
  matrix products  246 us (37%)
  blocking collectives  190 us (29%)
  waiting for transfers between devices  95.4 us (14%)
  other arithmetic  51 us (8%)
  starting transfers between devices  39.7 us (6%)
  local copies, waits for them, and re-layouts  37 us (6%)
    dot_general x36, matrix products, contract(): return jnp.einsum(form, left, right, precision=lax.Precision.HIGHEST)  246 us
    psum x1, blocking collectives, on_device(): gain_grad, short_grads = lax.psum((gain_part, filt_part), 'ctx')  69.2 us
    all_to_all x1, blocking collectives, on_device(): lax.all_to_all(chan_z, 'ctx', split_axis=1, concat_axis=0, tiled=True)  58.4 us
    all_to_all x1, blocking collectives, on_device(): lax.all_to_all(grad_conv.T, 'ctx', split_axis=0, concat_axis=1, tiled=True)  52.1 us
    all_to_all x1, waiting for transfers between devices, on_device(): lax.all_to_all(chan_du, 'ctx', split_axis=1, concat_axis=0, tiled=True)  26.7 us
    all_to_all x1, waiting for transfers between devices, on_device(): lax.all_to_all(long_filter.T, 'ctx', split_axis=0, concat_axis=1, tiled=T...  24.5 us
    all_to_all x1, waiting for transfers between devices, on_device(): lax.all_to_all(jnp.stack(jnp.split(mixed_in.T, lax.axis_size('ctx'), axis...  23.4 us
    all_to_all x1, waiting for transfers between devices, on_device(): lax.all_to_all(chan_dh, 'ctx', split_axis=1, concat_axis=0, tiled=True)  20.9 us
  transfers between devices with their start and end apart: 6, of which 4 were waited for; matrix products, arithmetic and copies ran while one was open for 11% of the time, Pallas kernels for 0%

profile of v1, /device:TPU:0, one launch (start us, length us, event | category | flops | bytes accessed | tf_op | source)
XLA Modules:
  0.0 660.6 jit_solution(4356061909955731773)
XLA Ops:
  8.4 6.6 all-to-all-start.1
  20.7 7.1 %fusion.6 = bf16[3,128,4096]{2,1,0:T(8,128)(2,1)S(1)} fusion(bf16[3,128,4096]{2,1,0:T(8,128)(2,1)S(1)} %copy-done.14, bf16[3,6,4096]{2,1,0:T(8,128)(2,1)} %collective-permute-done, f32[3,4096]{1,0:T(4,128)S(1)} %get-tuple-element.67, f32[3,4096]{1,0:T(4,128)S(1)} %get-tuple-element.68, f32[3,4096]{1,0:T(4,128)S(1)} %get-tuple-element.69, ...), kind=kLoop, calls=%fused_computation.26 | loop fusion | flops 61341696 | bytes 6782976 | tf_op jit(solution)/shard_map/convert_element_type | solution.py:98
  31.5 24.5 %all-to-all-done.1 = f32[16,256,128]{2,1,0:T(8,128)} async-done(((f32[16,256,128]{2,1,0:T(8,128)}), f32[16,256,128]{2,1,0:T(8,128)}, u32[]{:S(2)}, u32[]{:S(2)}) %all-to-all-start.1) | async-done | bytes 2097184 | tf_op jit(solution)/shard_map/all_to_all | solution.py:103
  56.0 11.7 %all-to-all-start = ((f32[16,256,128]{1,2,0:T(8,128)}), f32[16,256,128]{1,2,0:T(8,128)S(1)}, u32[]{:S(2)}, u32[]{:S(2)}) async-start(f32[16,256,128]{1,2,0:T(8,128)} %copy-done.16), calls=%async_computation | async-start | bytes 4194304 | tf_op jit(solution)/shard_map/all_to_all | solution.py:105
  71.2 8.3 %fusion.93 = f32[64,256,64]{1,0,2:T(8,128)} fusion(f32[256,32,64]{0,2,1:T(8,128)} %bitcast.298, f32[64,64]{0,1:T(8,128)S(1)} %fusion.166), kind=kOutput, calls=%fused_computation.147 | convolution fusion | flops 402653184 | bytes 6307840 | tf_op jit(solution)/shard_map/cnb,kn->ckb/dot_general | solution.py:20
  79.5 5.8 fusion.95
  85.3 23.4 %all-to-all-done = f32[16,256,128]{1,2,0:T(8,128)S(1)} async-done(((f32[16,256,128]{1,2,0:T(8,128)}), f32[16,256,128]{1,2,0:T(8,128)S(1)}, u32[]{:S(2)}, u32[]{:S(2)}) %all-to-all-start) | async-done | bytes 2097184 | tf_op jit(solution)/shard_map/all_to_all | solution.py:105
  108.7 5.8 fusion.97
  114.5 9.0 %add_bitcast_fusion.1 = (f32[256,64,64]{0,1,2:T(8,128)S(1)}, f32[256,64,64]{0,1,2:T(8,128)S(1)}, f32[256,64,64]{0,1,2:T(8,128)S(1)}, f32[256,64,64]{0,1,2:T(8,128)S(1)}) fusion(f32[64,256,64]{1,0,2:T(8,128)} %fusion.95, f32[64,256,64]{1,0,2:T(8,128)} %fusion.93, f32[64,64]{0,1:T(8,128)S(1)} %get-tuple-element.73, f32[64,64]{0,1:T(8,128)S(1)} %get-tuple-element.74, ...), kind=kOutput, calls=%fused_computation.75 | convolution fusion | flops 417333248 | bytes 31539200 | tf_op jit(solution)/shard_map/cnb,kn->ckb/dot_general | solution.py:20
  123.5 6.4 fusion.41
  129.9 6.9 %fusion.43 = f32[256,64,64]{0,2,1:T(8,128)S(1)} fusion(f32[256,64,64]{0,1,2:T(8,128)S(1)} %get-tuple-element.45), kind=kOutput, calls=%fused_computation.88 | convolution fusion | flops 805363712 | bytes 8388608 | tf_op jit(solution)/shard_map/ckb,bm->ckm/dot_general | solution.py:20
  136.8 7.2 %fusion.49 = f32[256,64,64]{0,2,1:T(8,128)} fusion(f32[256,64,64]{0,1,2:T(8,128)S(1)} %get-tuple-element.64), kind=kOutput, calls=%fused_computation.94 | convolution fusion | flops 805363712 | bytes 8388608 | tf_op jit(solution)/shard_map/ckb,bm->ckm/dot_general | solution.py:20
  144.0 6.5 fusion.51
  150.5 7.3 %fusion.73 = f32[256,64,64]{0,2,1:T(8,128)S(1)} fusion(f32[256,64,64]{0,2,1:T(8,128)S(1)} %fusion.41, f32[256,64,64]{0,1,2:T(8,128)S(1)} %get-tuple-element.44), kind=kOutput, calls=%fused_computation.120 | convolution fusion | flops 806412288 | bytes 12582912 | tf_op jit(solution)/shard_map/ckb,bm->ckm/dot_general | solution.py:20
  157.8 7.2 %fusion.70 = f32[256,64,64]{0,2,1:T(8,128)} fusion(f32[256,64,64]{0,2,1:T(8,128)S(1)} %fusion.43, f32[256,64,64]{0,1,2:T(8,128)S(1)} %get-tuple-element.44), kind=kOutput, calls=%fused_computation.119 | convolution fusion | flops 806412288 | bytes 12582912 | tf_op jit(solution)/shard_map/ckb,bm->ckm/dot_general | solution.py:20
  165.0 7.2 %fusion.64 = f32[256,64,64]{0,2,1:T(8,128)} fusion(f32[256,64,64]{0,2,1:T(8,128)S(1)} %fusion.51, f32[256,64,64]{0,1,2:T(8,128)S(1)} %get-tuple-element.65), kind=kOutput, calls=%fused_computation.117 | convolution fusion | flops 806412288 | bytes 12582912 | tf_op jit(solution)/shard_map/ckb,bm->ckm/dot_general | solution.py:20
  172.3 11.9 %multiply_add_fusion.5 = (f32[256,64,64]{0,2,1:T(8,128)S(1)}, f32[256,64,64]{0,2,1:T(8,128)S(1)}, f32[256,64,64]{0,2,1:T(8,128)}) fusion(f32[256,64,64]{0,2,1:T(8,128)} %fusion.70, f32[256,64,64]{0,2,1:T(8,128)} %fusion.64, f32[256,64,64]{0,2,1:T(8,128)S(1)} %fusion.73, f32[256,64,64]{0,2,1:T(8,128)} %fusion.49, f32[256,64,64]{0,1,2:T(8,128)S(1)} %get-tuple-element.65), kind=kOutput, calls=%fused_computation.72 | convolution fusion | flops 812703744 | bytes 33554432 | tf_op jit(solution)/shard_map/ckb,bm->ckm/dot_general | solution.py:20
  193.0 4.8 convolution_subtract_fusion.2
  197.8 6.6 multiply_subtract_fusion.4
  204.3 4.5 fusion.29
  208.9 4.9 multiply_bitcast_fusion.2
  215.0 58.4 %all_to_all.94 = f32[256,16,128]{0,2,1:T(8,128)S(1)} all-to-all(f32[256,16,128]{0,2,1:T(8,128)S(1)} %bitcast.305), channel_id=1, replica_groups=mesh['ctx'=16,'ch'=2] {'ctx'}, dimensions={1} | all-to-all | bytes 4194304 | tf_op jit(solution)/shard_map/all_to_all | solution.py:113
  275.4 5.0 psum.28
  283.1 4.9 psum.29
  292.4 52.1 %all_to_all.95 = f32[16,256,128]{1,2,0:T(8,128)S(1)} all-to-all(f32[16,256,128]{1,2,0:T(8,128)S(1)} %bitcast.307), channel_id=1, replica_groups=mesh['ctx'=16,'ch'=2] {'ctx'}, dimensions={0} | all-to-all | bytes 4194304 | tf_op jit(solution)/shard_map/all_to_all | solution.py:126
  344.4 4.6 fusion.89
  349.0 6.0 add_bitcast_fusion
  355.0 6.9 %fusion.33 = f32[256,64,64]{0,2,1:T(8,128)S(1)} fusion(f32[256,64,64]{0,1,2:T(8,128)S(1)} %get-tuple-element.41), kind=kOutput, calls=%fused_computation.78 | convolution fusion | flops 805363712 | bytes 8388608 | tf_op jit(solution)/shard_map/ckb,bm->ckm/dot_general | solution.py:20
  361.9 7.2 %fusion.35 = f32[256,64,64]{0,2,1:T(8,128)} fusion(f32[256,64,64]{0,1,2:T(8,128)S(1)} %get-tuple-element.41), kind=kOutput, calls=%fused_computation.80 | convolution fusion | flops 805363712 | bytes 8388608 | tf_op jit(solution)/shard_map/ckb,bm->ckm/dot_general | solution.py:20
  369.1 7.3 %fusion.79 = f32[256,64,64]{0,2,1:T(8,128)} fusion(f32[256,64,64]{0,2,1:T(8,128)S(1)} %fusion.33, f32[256,64,64]{0,1,2:T(8,128)S(1)} %get-tuple-element.40), kind=kOutput, calls=%fused_computation.122 | convolution fusion | flops 806412288 | bytes 12582912 | tf_op jit(solution)/shard_map/ckb,bm->ckm/dot_general | solution.py:20
  376.4 21.4 %multiply_subtract_fusion.1 = (f32[256,64,64]{0,2,1:T(8,128)}, f32[256,64,64]{0,2,1:T(8,128)}, f32[256,64,64]{0,2,1:T(8,128)}, f32[256,64,64]{0,2,1:T(8,128)}) fusion(f32[256,64,64]{0,2,1:T(8,128)} %get-tuple-element.66, f32[256,64,64]{0,2,1:T(8,128)} %fusion.64, f32[256,64,64]{0,2,1:T(8,128)} %fusion.79, f32[256,64,64]{0,2,1:T(8,128)} %copy-done.7, ...), kind=kOutput, calls=%fused_computation.62 | convolution fusion | flops 818995200 | bytes 46137344 | tf_op jit(solution)/shard_map/ckb,bm->ckm/dot_general | solution.py:20
  397.8 8.4 %fusion.139 = f32[256,64,64]{0,2,1:T(8,128)} fusion(f32[256,64,64]{0,2,1:T(8,128)} %get-tuple-element.26), kind=kOutput, calls=%fused_computation.225 | convolution fusion | flops 805363712 | bytes 8388608 | tf_op jit(solution)/shard_map/ckb,bm->ckm/dot_general | solution.py:20
  410.4 5.8 convolution_subtract_fusion
  424.6 5.6 convolution_subtract_fusion.1
  430.2 5.8 convolution_add_fusion.1
  436.0 11.6 %multiply_subtract_fusion = (f32[256,64,64]{0,2,1:T(8,128)}, f32[256,64,64]{0,2,1:T(8,128)}, f32[256,64,64]{0,2,1:T(8,128)}, f32[256,64,64]{0,2,1:T(8,128)S(1)}) fusion(f32[256,64,64]{0,2,1:T(8,128)} %convolution_subtract_fusion, f32[64,64]{1,0:T(8,128)S(1)} %copy.79, f32[64,64]{1,0:T(8,128)S(1)} %copy.78, f32[256,64,64]{0,2,1:T(8,128)} %convolution_subtract_fusion.1, ...), kind=kOutput, calls=%fused_computation.61 | convolution fusion | flops 818995200 | bytes 37781504 | tf_op jit(solution)/shard_map/ckb,bm->ckm/dot_general | solution.py:20
  447.6 7.4 %fusion.25 = f32[32,256,64]{1,0,2:T(8,128)S(1)} fusion(f32[256,64,64]{0,2,1:T(8,128)} %get-tuple-element.62, f32[64,64]{0,1:T(8,128)S(1)} %fusion.166), kind=kOutput, calls=%fused_computation.52 | convolution fusion | flops 402653184 | bytes 6307840 | tf_op jit(solution)/shard_map/ckb,kn->cnb/dot_general | solution.py:20
  455.0 4.7 multiply_bitcast_fusion.1
  462.3 5.4 all-to-all-start.4
  467.7 7.1 %fusion.21 = f32[32,256,64]{1,0,2:T(8,128)S(1)} fusion(f32[256,64,64]{0,2,1:T(8,128)} %get-tuple-element.37, f32[64,64]{0,1:T(8,128)S(1)} %fusion.166), kind=kOutput, calls=%fused_computation.48 | convolution fusion | flops 402653184 | bytes 6307840 | tf_op jit(solution)/shard_map/ckb,kn->cnb/dot_general | solution.py:20
  474.8 4.7 multiply_bitcast_fusion
  482.0 26.7 %all-to-all-done.4 = f32[256,16,128]{0,2,1:T(8,128)} async-done(((f32[256,16,128]{0,2,1:T(8,128)}), f32[256,16,128]{0,2,1:T(8,128)}, u32[]{:S(2)}, u32[]{:S(2)}) %all-to-all-start.4) | async-done | bytes 2097184 | tf_op jit(solution)/shard_map/all_to_all | solution.py:136
  508.7 11.5 %all-to-all-start.5 = ((f32[256,16,128]{0,2,1:T(8,128)}), f32[256,16,128]{0,2,1:T(8,128)}, u32[]{:S(2)}, u32[]{:S(2)}) async-start(f32[256,16,128]{0,2,1:T(8,128)} %bitcast.303), calls=%async_computation.5 | async-start | bytes 4194304 | tf_op jit(solution)/shard_map/all_to_all | solution.py:137
  525.6 8.5 %fusion.12 = (f32[3,4096]{1,0:T(4,128)S(1)}, f32[3,4096]{1,0:T(4,128)S(1)}, f32[3,4096]{1,0:T(4,128)S(1)}, f32[3,4096]{1,0:T(4,128)S(1)}, f32[3,4096]{1,0:T(4,12...) fusion(bf16[3,128,4096]{2,1,0:T(8,128)(2,1)S(1)} %copy-done.15, bf16[3,6,4096]{2,1,0:T(8,128)(2,1)} %collective-permute-done, ...), kind=kLoop, calls=%fused_computation.32 | loop fusion | flops 64401408 | bytes 9928704 | tf_op jit(solution)/shard_map/reduce_sum | solution.py:152
  540.3 20.9 %all-to-all-done.5 = f32[256,16,128]{0,2,1:T(8,128)} async-done(((f32[256,16,128]{0,2,1:T(8,128)}), f32[256,16,128]{0,2,1:T(8,128)}, u32[]{:S(2)}, u32[]{:S(2)}) %all-to-all-start.5) | async-done | bytes 2097184 | tf_op jit(solution)/shard_map/all_to_all | solution.py:137
  567.3 69.2 %all-reduce = (f32[3,7,256]{2,0,1:T(4,128)S(1)}, f32[4096]{0:T(1024)}) all-reduce(f32[3,7,256]{2,0,1:T(4,128)S(1)} %constant_dynamic-update-slice_fusion, f32[4096]{0:T(1024)S(1)} %get-tuple-element.22), channel_id=1, replica_groups=mesh['ctx'=16,'ch'=2] {'ctx'}, use_global_device_ids=true, to_apply=%region_18.19 | all-reduce | flops 9472 | bytes 75776 | tf_op jit(solution)/shard_map/psum | solution.py:155
  637.2 4.7 pad_maximum_fusion
  641.9 18.4 %fusion.15 = bf16[3,128,4096]{2,1,0:T(8,128)(2,1)} fusion(f32[3,134,4096]{2,1,0:T(8,128)} %pad_maximum_fusion, f32[3,4096]{1,0:T(4,128)S(1)} %copy-done.18, f32[3,4096]{1,0:T(4,128)S(1)} %copy-done.20, f32[3,4096]{1,0:T(4,128)S(1)} %copy-done.22, f32[3,4096]{1,0:T(4,128)S(1)} %copy-done.24, f32[3,4096]{1,0:T(4,128)S(1)} %copy-done.26, ...), kind=kLoop, calls=%fused_computation.36 | loop fusion | flops 25165824 | bytes 47529984 | tf_op jit(solution)/shard_map/convert_element_type | solution.py:156
  (145 shorter events, 75.3 us)
Async XLA Ops:
  2.3 12.7 %copy-start.32 = (f32[3,7,256]{2,1,0:T(8,128)S(1)}, f32[3,7,256]{2,1,0:T(8,128)}, u32[]{:S(2)}) copy-start(f32[3,7,256]{2,1,0:T(8,128)} %param.6) | copy-start | bytes 64516
  2.3 18.4 %collective-permute-start = (bf16[3,6,4096]{2,1,0:T(8,128)(2,1)}, bf16[3,6,4096]{2,1,0:T(8,128)(2,1)}, u32[]{:S(2)}, u32[]{:S(2)}) collective-permute-start(bf16[3,6,4096]{2,1,0:T(8,128)(2,1)} %slice.123), channel_id=1, source_target_pairs={{0,2},{2,4},{4,6},{6,8},{8,10},{10,12},{12,14},{14,16},{16,18},{18... | collective-permute-start | bytes 442376 | tf_op jit(solution)/shard_map/ppermute | solution.py:16
  8.4 47.6 %all-to-all-start.1 = ((f32[16,256,128]{2,1,0:T(8,128)}), f32[16,256,128]{2,1,0:T(8,128)}, u32[]{:S(2)}, u32[]{:S(2)}) async-start(f32[16,256,128]{2,1,0:T(8,128)} %bitcast.30), calls=%async_computation.1 | async-start | bytes 4194304 | tf_op jit(solution)/shard_map/all_to_all | solution.py:103
  15.0 5.8 copy-start.14
  20.4 9.3 %copy-start.17 = (f32[3,4096]{1,0:T(4,128)}, f32[3,4096]{1,0:T(4,128)S(1)}, u32[]{:S(2)}) copy-start(f32[3,4096]{1,0:T(4,128)S(1)} %get-tuple-element.67) | copy-start | bytes 147460
  20.5 9.3 %copy-start.19 = (f32[3,4096]{1,0:T(4,128)}, f32[3,4096]{1,0:T(4,128)S(1)}, u32[]{:S(2)}) copy-start(f32[3,4096]{1,0:T(4,128)S(1)} %get-tuple-element.68) | copy-start | bytes 147460
  20.5 9.2 %copy-start.21 = (f32[3,4096]{1,0:T(4,128)}, f32[3,4096]{1,0:T(4,128)S(1)}, u32[]{:S(2)}) copy-start(f32[3,4096]{1,0:T(4,128)S(1)} %get-tuple-element.69) | copy-start | bytes 147460
  20.5 9.2 %copy-start.23 = (f32[3,4096]{1,0:T(4,128)}, f32[3,4096]{1,0:T(4,128)S(1)}, u32[]{:S(2)}) copy-start(f32[3,4096]{1,0:T(4,128)S(1)} %get-tuple-element.70) | copy-start | bytes 147460
  20.6 9.2 %copy-start.25 = (f32[3,4096]{1,0:T(4,128)}, f32[3,4096]{1,0:T(4,128)S(1)}, u32[]{:S(2)}) copy-start(f32[3,4096]{1,0:T(4,128)S(1)} %get-tuple-element.71) | copy-start | bytes 147460
  20.6 9.2 %copy-start.27 = (f32[3,4096]{1,0:T(4,128)}, f32[3,4096]{1,0:T(4,128)S(1)}, u32[]{:S(2)}) copy-start(f32[3,4096]{1,0:T(4,128)S(1)} %get-tuple-element.72) | copy-start | bytes 147460
  20.7 9.1 %copy-start.29 = (f32[3,1,4096]{2,0,1:T(4,128)}, f32[3,1,4096]{2,0,1:T(4,128)S(1)}, u32[]{:S(2)}) copy-start(f32[3,1,4096]{2,0,1:T(4,128)S(1)} %copy.194) | copy-start | bytes 147460
  27.8 1.7 copy-start.8
  30.1 1.4 copy-start.16
  56.0 52.7 %all-to-all-start = ((f32[16,256,128]{1,2,0:T(8,128)}), f32[16,256,128]{1,2,0:T(8,128)S(1)}, u32[]{:S(2)}, u32[]{:S(2)}) async-start(f32[16,256,128]{1,2,0:T(8,128)} %copy-done.16), calls=%async_computation | async-start | bytes 4194304 | tf_op jit(solution)/shard_map/all_to_all | solution.py:105
  71.2 8.3 %copy-start.12 = (f32[256,16,128]{0,2,1:T(8,128)S(1)}, f32[256,16,128]{0,2,1:T(8,128)}, u32[]{:S(2)}) copy-start(f32[256,16,128]{0,2,1:T(8,128)} %copy.69) | copy-start | bytes 6291460
  157.8 14.5 %copy-start.7 = (f32[256,64,64]{0,2,1:T(8,128)}, f32[256,64,64]{0,2,1:T(8,128)S(1)}, u32[]{:S(2)}) copy-start(f32[256,64,64]{0,2,1:T(8,128)S(1)} %fusion.73) | copy-start | bytes 12582916
  215.0 60.0 %copy-start.9 = (bf16[3,128,4096]{2,1,0:T(8,128)(2,1)S(1)}, bf16[3,128,4096]{2,1,0:T(8,128)(2,1)}, u32[]{:S(2)}) copy-start(bf16[3,128,4096]{2,1,0:T(8,128)(2,1)} %copy-done.8) | copy-start | bytes 9437188
  273.4 7.0 %copy-start.31 = (f32[4096]{0:T(1024)S(1)}, f32[4096]{0:T(1024)}, u32[]{:S(2)}) copy-start(f32[4096]{0:T(1024)} %param.8) | copy-start | bytes 49156
  273.6 1.3 copy-start.11
  355.0 14.1 %copy-start.6 = (f32[256,64,64]{0,1,2:T(8,128)}, f32[256,64,64]{0,1,2:T(8,128)S(1)}, u32[]{:S(2)}) copy-start(f32[256,64,64]{0,1,2:T(8,128)S(1)} %get-tuple-element.40) | copy-start | bytes 12582916
  397.8 8.4 %copy-start.2 = (f32[256,64,64]{0,2,1:T(8,128)S(1)}, f32[256,64,64]{0,2,1:T(8,128)}, u32[]{:S(2)}) copy-start(f32[256,64,64]{0,2,1:T(8,128)} %get-tuple-element.27) | copy-start | bytes 12582916
  406.2 4.2 copy-start.5
  410.4 5.8 copy-start.3
  416.2 4.2 copy-start.4
  462.3 46.4 %all-to-all-start.4 = ((f32[256,16,128]{0,2,1:T(8,128)}), f32[256,16,128]{0,2,1:T(8,128)}, u32[]{:S(2)}, u32[]{:S(2)}) async-start(f32[256,16,128]{0,2,1:T(8,128)} %bitcast.304), calls=%async_computation.4 | async-start | bytes 4194304 | tf_op jit(solution)/shard_map/all_to_all | solution.py:136
  467.7 7.1 %copy-start.13 = (f32[256,64,64]{0,2,1:T(8,128)S(1)}, f32[256,64,64]{0,2,1:T(8,128)}, u32[]{:S(2)}) copy-start(f32[256,64,64]{0,2,1:T(8,128)} %get-tuple-element.36) | copy-start | bytes 12582916
  508.7 52.5 %all-to-all-start.5 = ((f32[256,16,128]{0,2,1:T(8,128)}), f32[256,16,128]{0,2,1:T(8,128)}, u32[]{:S(2)}, u32[]{:S(2)}) async-start(f32[256,16,128]{0,2,1:T(8,128)} %bitcast.303), calls=%async_computation.5 | async-start | bytes 4194304 | tf_op jit(solution)/shard_map/all_to_all | solution.py:137
  520.1 2.5 copy-start.10
  522.7 2.9 copy-start.15
  523.2 10.9 %copy-start = (f32[1,128,4096]{2,1,0:T(8,128)}, f32[1,128,4096]{2,1,0:T(8,128)S(1)}, u32[]{:S(2)}) copy-start(f32[1,128,4096]{2,1,0:T(8,128)S(1)} %get-tuple-element.53) | copy-start | bytes 6291460
  523.2 10.9 %copy-start.1 = (f32[1,128,4096]{2,1,0:T(8,128)}, f32[1,128,4096]{2,1,0:T(8,128)S(1)}, u32[]{:S(2)}) copy-start(f32[1,128,4096]{2,1,0:T(8,128)S(1)} %get-tuple-element.54) | copy-start | bytes 6291460
  538.9 98.3 %collective-permute-start.1 = (f32[3,6,4096]{2,1,0:T(8,128)S(1)}, f32[3,6,4096]{2,1,0:T(8,128)S(1)}, u32[]{:S(2)}, u32[]{:S(2)}) collective-permute-start(f32[3,6,4096]{2,1,0:T(8,128)S(1)} %slice.169), channel_id=1, source_target_pairs={{2,0},{4,2},{6,4},{8,6},{10,8},{12,10},{14,12},{16,14},{18,16},{20... | collective-permute-start | bytes 884744 | tf_op jit(solution)/shard_map/ppermute | solution.py:16
  637.2 4.7 copy-start.18
  637.2 4.7 copy-start.20
  637.2 4.7 copy-start.22
  637.2 4.7 copy-start.24
  637.2 4.7 copy-start.26
  637.2 4.7 copy-start.28
  637.2 4.7 copy-start.30
